TPU v7x, 32 devices: a whole 2x2x4 slice. The times are simulated.
32 devices in a mesh: dp: 2 (over core), rows: 4 (over y, x), cols: 4 (over z).
Axes of the slice: x: 2, y: 2, z: 4, core: 2. Of those that a mesh axis runs over, the one named last changes fastest.
Arguments:
- tokens: bfloat16 [8192, 2048], P(('dp', 'rows', 'cols')), may hold values from -6 to 6
- attention_gain: float32 [2048], replicated, may hold values from 0.5 to 1.5
- mlp_gain: float32 [2048], replicated, may hold values from 0.5 to 1.5
- w_query: bfloat16 [2048, 2048], P('rows', 'cols'), may hold values from -0.25 to 0.25
- w_key: bfloat16 [2048, 256], P('rows'), may hold values from -0.125 to 0.125
- w_value: bfloat16 [2048, 256], P('rows'), may hold values from -0.125 to 0.125
- w_out: bfloat16 [2048, 2048], P(None, 'rows'), may hold values from -0.5 to 0.5
- w_gate: bfloat16 [2048, 5632], P('rows', 'cols'), may hold values from -0.125 to 0.125
- w_up: bfloat16 [2048, 5632], P('rows', 'cols'), may hold values from -0.125 to 0.125
- w_down: bfloat16 [5632, 2048], P('cols', 'rows'), may hold values from -0.078125 to 0.078125
- segment_ids: int32 [8, 1024], P(('dp', 'rows')), may hold values from 0 to 3, never falling along the last dimension, each value on 1 to 512 neighbouring positions
- skip_mask: int32 [8], P(('dp', 'rows')), may hold values 0 or 1
- cotangent: float32 [8192, 2048], P(('dp', 'rows', 'cols')), may hold values from -6 to 6
Outputs:
- output: bfloat16 [8192, 2048], P(('dp', 'rows', 'cols'))
- input_grad: float32 [8192, 2048], P(('dp', 'rows', 'cols'))
- attention_gain_grad: float32 [2048], replicated
- mlp_gain_grad: float32 [2048], replicated
- query_grad: float32 [2048, 2048], P(('dp', 'rows'), 'cols')
- key_grad: float32 [2048, 256], replicated
- value_grad: float32 [2048, 256], replicated
- out_grad: float32 [2048, 2048], P('cols', ('dp', 'rows'))
- gate_grad: float32 [2048, 5632], P(('dp', 'rows'), 'cols')
- up_grad: float32 [2048, 5632], P(('dp', 'rows'), 'cols')
- down_grad: float32 [5632, 2048], P('cols', ('dp', 'rows'))
Inputs may be any that keep to these rules, and one draw needn't show every extreme that they name: `segment_ids`: segment numbers never fall along a sequence of 1024 tokens; each sequence holds max(4, 4) documents, a document holds at most 512 tokens, and some document holds exactly that many.
All inputs are finite; a program needn't handle non-finite values. No bound on the sum of `skip_mask` on one device may be relied on, other than what follows from the above.
Results may differ from a plain program's by a relative error of at most 0.014.
Values may be sent and summed in bfloat16 or wider, within the bound.
No kernel may reach another device: no remote copies, remote signals or barrier semaphores. Data moves between devices by JAX's collectives and lax.ppermute only.
A program may use at most 320 MiB of HBM per device.

v0:
```python
import jax
import jax.numpy as jnp
from jax import lax
from jax.sharding import PartitionSpec as P

HEADS = 16
KV_HEADS = 2
HEAD_DIM = 128
epsilon = 1e-05
negative = -1e30
rope_base = 10000.0
bf16 = jnp.bfloat16
f32 = jnp.float32


def dot(left, right, dims):
    return lax.dot_general(
        left, right, ((dims[:1], dims[1:]), ((), ())), preferred_element_type=f32
    )


def nn(left, right):
    return dot(left, right, (1, 0))


def nt(left, right):
    return dot(left, right, (1, 1))


def tn(left, right):
    return dot(left, right, (0, 0))


def after(value, *earlier):
    return lax.optimization_barrier((value,) + earlier)[0]


def xor_blocks(blocks, index):
    bit = 1
    while bit < len(blocks):
        swap = index & bit != 0
        blocks = [jnp.where(swap, blocks[j ^ bit], blocks[j]) for j in range(len(blocks))]
        bit *= 2
    return blocks


def xor_order(value, index, count, axis):
    return jnp.concatenate(xor_blocks(jnp.split(value, count, axis), index), axis)


def rotary_tables(positions):
    half = HEAD_DIM // 2
    frequency = rope_base ** (-2.0 * jnp.arange(half, dtype=f32) / HEAD_DIM)
    angles = positions.astype(f32)[:, None] * frequency[None, :]
    return (jnp.cos(angles)[:, None, :], jnp.sin(angles)[:, None, :])


def rotate(values, cosine, sine, direction):
    heads = values.reshape(values.shape[0], -1, HEAD_DIM)
    half = HEAD_DIM // 2
    a, b = (heads[..., :half], heads[..., half:])
    s = sine * direction
    turned = jnp.concatenate([a * cosine - b * s, b * cosine + a * s], axis=-1)
    return turned.reshape(values.shape)


def norm_factor(values):
    return lax.rsqrt(jnp.mean(values * values, axis=-1, keepdims=True) + epsilon)


def norm_back(grad, values, factor, gain):
    y = grad * gain
    pulled = factor * y - values * factor**3 * jnp.mean(y * values, axis=-1, keepdims=True)
    return (pulled, jnp.sum(grad * values * factor, axis=0))


def local(
    tokens,
    attention_gain,
    mlp_gain,
    w_query,
    w_key,
    w_value,
    w_out,
    w_gate,
    w_up,
    w_down,
    segment_ids,
    skip_mask,
    cotangent,
):
    cols, rows = (lax.axis_size("cols"), lax.axis_size("rows"))
    c, r, d = (lax.axis_index("cols"), lax.axis_index("rows"), lax.axis_index("dp"))
    own, width = tokens.shape
    sequences, length = segment_ids.shape
    place = 2 * r + d
    blocks = 2 * rows
    step = width // blocks
    scale = HEAD_DIM ** (-0.5)

    def to_rows(value, a):
        return lax.ppermute(value, "rows", [(i, i ^ a) for i in range(rows)])

    def to_core(value):
        return lax.ppermute(value, "dp", [(0, 1), (1, 0)])

    def to_cols(value, k):
        return lax.ppermute(value, "cols", [(i, (i + k) % cols) for i in range(cols)])

    def along(value, k):
        return lax.ppermute(value, "cols", [(i, i + k) for i in range(cols) if 0 <= i + k < cols])

    def to_xor_cols(value, k):
        return lax.ppermute(value, "cols", [(i, i ^ k) for i in range(cols)])

    def fetch_rows(piece, first):
        if rows != 4:
            return [piece] + [to_rows(piece, a) for a in range(1, rows)]
        other = 3 - first
        near = to_rows(piece, first)
        far = to_rows(piece, other)
        both = to_rows(near, other)
        got = [piece, None, None, both]
        got[first], got[other] = (near, far)
        return got

    def with_core(got, own_other):
        pairs = []
        for j, piece in enumerate(got):
            pairs += [piece, own_other if j == 0 else to_core(piece)]
        return pairs

    def halves(weight, axis):
        low, high = jnp.split(weight, 2, axis)
        return (jnp.where(d == 0, low, high), jnp.where(d == 0, high, low))

    inputs = xor_order(tokens, place, blocks, 1).astype(f32)
    upstream = xor_order(cotangent, place, blocks, 1)
    gain_one = xor_order(attention_gain, place, blocks, 0)
    gain_two = xor_order(mlp_gain, place, blocks, 0)
    sequence = c * own // length
    start = c * own % length
    keep = (1 - lax.dynamic_index_in_dim(skip_mask, sequence, 0, False)).astype(f32)
    feed_own = (keep * upstream).astype(bf16)
    kv_mine, kv_other = halves(jnp.concatenate([w_key, w_value], 1), 0)
    kv_got = fetch_rows(kv_mine, 1)
    kv_matrix = jnp.concatenate(with_core(kv_got, kv_other), 0)
    q_mine, _ = halves(w_query, 0)
    q_parts = [q_mine] + [to_xor_cols(q_mine, k) for k in range(1, cols)]
    q_mine = jnp.concatenate(xor_blocks(q_parts, c), 1)
    q_lo, q_hi = jnp.split(q_mine, 2, 0)
    q_lo_got = fetch_rows(after(q_lo, kv_got[1]), 1)
    q_hi_got = fetch_rows(after(q_hi, kv_got[1]), 2)
    q_got = [jnp.concatenate([lo, hi], 0) for lo, hi in zip(q_lo_got, q_hi_got)]
    q_pairs = []
    for piece in q_got:
        q_pairs += [piece, to_core(piece)]
    q_matrix = jnp.concatenate(q_pairs, 0)
    o_mine, o_other = halves(w_out, 1)
    o_mine = after(o_mine, q_lo_got[1], q_hi_got[2])
    o_lo, o_hi = jnp.split(o_mine, 2, 0)
    o_lo_got, o_hi_got = (fetch_rows(o_lo, 1), fetch_rows(o_hi, 2))
    o_got = [jnp.concatenate([lo, hi], 0) for lo, hi in zip(o_lo_got, o_hi_got)]
    o_matrix = jnp.concatenate(with_core(o_got, o_other), 1)
    g_mine, g_other = halves(w_gate, 0)
    u_mine, u_other = halves(w_up, 0)
    g_got = fetch_rows(after(g_mine, o_lo_got[1], o_hi_got[2]), 1)
    u_got = fetch_rows(after(u_mine, o_lo_got[1], o_hi_got[2]), 2)
    g_matrix = jnp.concatenate(with_core(g_got, g_other), 0)
    u_matrix = jnp.concatenate(with_core(u_got, u_other), 0)
    w_mine, w_other = halves(w_down, 1)
    w_mine = after(w_mine, g_got[1], u_got[2])
    w_lo, w_hi = jnp.split(w_mine, 2, 0)
    w_lo_got, w_hi_got = (fetch_rows(w_lo, 1), fetch_rows(w_hi, 2))
    w_got = [jnp.concatenate([lo, hi], 0) for lo, hi in zip(w_lo_got, w_hi_got)]
    d_matrix = jnp.concatenate(with_core(w_got, w_other), 1)
    factor_one = norm_factor(inputs)
    normed = (inputs * factor_one * gain_one).astype(bf16)
    cosine, sine = rotary_tables(start + jnp.arange(own))
    kv_pre = nn(normed, kv_matrix)
    kv_width = KV_HEADS * HEAD_DIM
    kv_own = jnp.concatenate(
        [rotate(kv_pre[:, :kv_width], cosine, sine, 1.0), kv_pre[:, kv_width:]], 1
    ).astype(bf16)
    reach = min(-(-(length // 2 - 1) // own), length // own - 1)
    kv_before = [along(kv_own, k) for k in range(reach, 0, -1)]
    kv_all = jnp.concatenate(kv_before + [kv_own], 0)
    span = (reach + 1) * own
    q_rows = rotate(nn(normed, q_matrix), cosine, sine, 1.0).astype(bf16)
    feeds = [after(feed_own, q_parts[1])]
    for k in range(1, cols):
        feeds.append(to_cols(feeds[-1], 1))
    ids = lax.dynamic_index_in_dim(segment_ids, sequence, 0, False)
    ids_padded = jnp.concatenate([jnp.full((reach * own,), -1, ids.dtype), ids])
    ids_keys = lax.dynamic_slice_in_dim(ids_padded, start, span, 0)
    ids_rows = ids_keys[reach * own :]
    allowed = (ids_rows[:, None] == ids_keys[None, :]) & (
        (reach * own + jnp.arange(own))[:, None] >= jnp.arange(span)[None, :]
    )
    share = HEADS // KV_HEADS
    q_heads = q_rows.reshape(own, KV_HEADS, share, HEAD_DIM)
    k_heads = kv_all[:, :kv_width].reshape(span, KV_HEADS, HEAD_DIM)
    v_heads = kv_all[:, kv_width:].reshape(span, KV_HEADS, HEAD_DIM)

    def ein(form, a, b):
        return jnp.einsum(form, a, b, preferred_element_type=f32)

    scores = ein("bghe,kge->ghbk", q_heads, k_heads) * scale
    scores = jnp.where(allowed[None, None], scores, negative)
    top = jnp.max(scores, -1, keepdims=True)
    exponent = jnp.exp(scores - top)
    probs = exponent / jnp.sum(exponent, -1, keepdims=True)
    attend = probs.astype(bf16)
    mixed = ein("ghbk,kge->bghe", attend, v_heads).reshape(own, width).astype(bf16)
    branch = nn(mixed, o_matrix)
    middle = inputs + keep * branch
    factor_two = norm_factor(middle)
    hidden_own = (middle * factor_two * gain_two).astype(bf16)
    chunks = [hidden_own]
    for k in range(1, cols):
        chunks.append(to_cols(chunks[-1], 1))
    hiddens, gate_backs, up_backs, feed_parts, in_parts = ({}, {}, {}, {}, {})
    carry_in = None
    for k in list(range(1, cols)) + [0]:
        gate = nn(chunks[k], g_matrix)
        up = nn(chunks[k], u_matrix)
        back = nt(feeds[k], d_matrix)
        s = jax.nn.sigmoid(gate)
        hiddens[k] = (gate * s * up).astype(bf16)
        gate_backs[k] = (back * up * s * (1.0 + gate * (1.0 - s))).astype(bf16)
        up_backs[k] = (back * gate * s).astype(bf16)
        part = nt(gate_backs[k], g_matrix) + nt(up_backs[k], u_matrix)
        if carry_in is not None:
            part = part + carry_in.astype(f32)
        if k != 0:
            carry_in = to_cols(part.astype(bf16), 1)
        else:
            hidden_in_back = part
    order = list(range(cols))
    h_all = jnp.concatenate([chunks[k] for k in order], 0)
    f_all = jnp.concatenate([feeds[k] for k in order], 0)
    hid_all = jnp.concatenate([hiddens[k] for k in order], 0)
    gb_all = jnp.concatenate([gate_backs[k] for k in order], 0)
    ub_all = jnp.concatenate([up_backs[k] for k in order], 0)
    down_part = tn(hid_all, f_all).astype(bf16)
    gate_part = tn(h_all, gb_all).astype(bf16)
    up_part = tn(h_all, ub_all).astype(bf16)
    from_norm, mlp_gain_part = norm_back(hidden_in_back, middle, factor_two, gain_two)
    middle_grad = upstream + from_norm
    branch_back = (keep * middle_grad).astype(bf16)
    mixed_back = nt(branch_back, o_matrix).astype(bf16)
    out_part = tn(mixed, branch_back).astype(bf16)
    carry_out = None
    for k in list(range(1, cols)) + [0]:
        part = nn(after(hiddens[k], hidden_in_back), d_matrix)
        if carry_out is not None:
            part = part + carry_out.astype(f32)
        if k != 0:
            carry_out = to_cols(part.astype(bf16), 1)
    feed_values = part
    output = (middle + keep * feed_values).astype(bf16)
    mb_heads = mixed_back.reshape(own, KV_HEADS, share, HEAD_DIM)
    weight_back = ein("bghe,kge->ghbk", mb_heads, v_heads)
    inner = jnp.sum(weight_back * probs, -1, keepdims=True)
    score_back = (probs * (weight_back - inner)).astype(bf16)
    q_turned = ein("ghbk,kge->bghe", score_back, k_heads).reshape(own, width) * scale
    k_turned = ein("ghbk,bghe->kge", score_back, q_heads).reshape(span, kv_width) * scale
    v_turned = ein("ghbk,bghe->kge", attend, mb_heads).reshape(span, kv_width)
    kv_turned = jnp.concatenate([k_turned, v_turned], 1)
    kv_back_pre = kv_turned[reach * own :]
    for k in range(1, reach + 1):
        part = kv_turned[(reach - k) * own : (reach - k + 1) * own].astype(bf16)
        kv_back_pre = kv_back_pre + along(part, -k).astype(f32)
    q_back = rotate(q_turned, cosine, sine, -1.0).astype(bf16)
    kv_back = jnp.concatenate(
        [rotate(kv_back_pre[:, :kv_width], cosine, sine, -1.0), kv_back_pre[:, kv_width:]], 1
    ).astype(bf16)
    q_part = tn(normed, q_back).astype(bf16)
    normed_back = nt(q_back, q_matrix) + nt(kv_back, kv_matrix)
    from_norm, attention_gain_part = norm_back(normed_back, inputs, factor_one, gain_one)
    input_grad = xor_order(middle_grad + from_norm, place, blocks, 1)
    kv_part = tn(normed, kv_back).astype(bf16)

    def scatter(part, axis, first):
        parts = xor_blocks(jnp.split(part, blocks, axis), place ^ d * rows + r)
        keep_half = jnp.concatenate(parts[:rows], axis)
        send_half = jnp.concatenate(parts[rows:], axis)
        half = keep_half.astype(f32) + to_core(send_half).astype(f32)
        pieces = jnp.split(half, rows, axis)
        if rows != 4:
            total = pieces[0]
            for a in range(1, rows):
                total = total + to_rows(pieces[a].astype(bf16), a).astype(f32)
            return total
        other = 3 - first
        near = to_rows(jnp.concatenate([pieces[first], pieces[3]], axis).astype(bf16), first)
        near = jnp.split(near, 2, axis)
        mine = pieces[0] + near[0].astype(f32)
        theirs = pieces[other] + near[1].astype(f32)
        return mine + to_rows(theirs.astype(bf16), other).astype(f32)

    gate_grad = scatter(gate_part, 0, 1)
    up_grad = scatter(up_part, 0, 2)
    down_lo, down_hi = jnp.split(down_part, 2, 0)
    down_grad = jnp.concatenate([scatter(down_lo, 1, 1), scatter(down_hi, 1, 2)], 0)

    def scatter_cols(total, axis):
        pieces = xor_blocks(jnp.split(total.astype(bf16), cols, axis), c)
        result = pieces[0].astype(f32)
        for k in range(1, cols):
            result = result + to_xor_cols(pieces[k], k).astype(f32)
        return result

    out_lo, out_hi = jnp.split(out_part, 2, 0)
    out_sum = jnp.concatenate([scatter(out_lo, 1, 1), scatter(out_hi, 1, 2)], 0)
    out_grad = scatter_cols(out_sum, 0)
    q_lo, q_hi = jnp.split(q_part, 2, 1)
    q_sum = jnp.concatenate([scatter(q_lo, 0, 1), scatter(q_hi, 0, 2)], 1)
    query_grad = scatter_cols(q_sum, 1)
    kv_sum = scatter(kv_part, 0, 1).astype(bf16)
    total = kv_sum.astype(f32)
    for k in range(1, cols):
        total = total + to_xor_cols(kv_sum, k).astype(f32)
    total = total.astype(bf16)
    found = fetch_rows(total, 1)
    found = found + [to_core(x) for x in found]
    found = jnp.concatenate(xor_blocks(found, d * rows + r), 0).astype(f32)
    key_grad, value_grad = (found[:, :kv_width], found[:, kv_width:])
    gains = jnp.stack([attention_gain_part, mlp_gain_part])
    gains = lax.psum(xor_order(gains, place, blocks, 1), ("dp", "rows", "cols"))
    return (
        xor_order(output, place, blocks, 1),
        input_grad,
        gains[0],
        gains[1],
        query_grad,
        key_grad,
        value_grad,
        out_grad,
        gate_grad,
        up_grad,
        down_grad,
    )


def solution(mesh):
    return jax.shard_map(
        local,
        mesh=mesh,
        in_specs=(
            P(("dp", "rows", "cols"), None),
            P(),
            P(),
            P("rows", "cols"),
            P("rows", None),
            P("rows", None),
            P(None, "rows"),
            P("rows", "cols"),
            P("rows", "cols"),
            P("cols", "rows"),
            P(("dp", "rows"), None),
            P(("dp", "rows")),
            P(("dp", "rows", "cols"), None),
        ),
        out_specs=(
            P(("dp", "rows", "cols"), None),
            P(("dp", "rows", "cols"), None),
            P(),
            P(),
            P(("dp", "rows"), "cols"),
            P(),
            P(),
            P("cols", ("dp", "rows")),
            P(("dp", "rows"), "cols"),
            P(("dp", "rows"), "cols"),
            P("cols", ("dp", "rows")),
        ),
        check_vma=False,
    )
```

profile of v0, /device:TPU:0, one launch (start us, length us, event | category | flops | bytes accessed | tf_op | source)
XLA Modules:
  0.0 911.4 jit_solution(14802513030163577752)
XLA Ops:
  25.5 9.0 collective-permute-done.9
  57.7 15.1 %collective-permute-done.16 = bf16[128,2048]{1,0:T(8,128)(2,1)} collective-permute-done((bf16[128,2048]{1,0:T(8,128)(2,1)}, bf16[128,2048]{1,0:T(8,128)(2,1)}, u32[]{:S(2)}, u32[]{:S(2)}) %collective-permute-start.16) | collective-permute-done | bytes 524320 | tf_op jit(solution)/shard_map/ppermute | solution.py:102
  141.2 11.1 %collective-permute-done.28 = bf16[1024,256]{1,0:T(8,128)(2,1)S(1)} collective-permute-done((bf16[1024,256]{1,0:T(8,128)(2,1)}, bf16[1024,256]{1,0:T(8,128)(2,1)S(1)}, u32[]{:S(2)}, u32[]{:S(2)}) %collective-permute-start.28) | collective-permute-done | bytes 524320 | tf_op jit(solution)/shard_map/ppermute | solution.py:102
  157.3 9.7 %collective-permute-done.36 = bf16[256,1408]{1,0:T(8,128)(2,1)S(1)} collective-permute-done((bf16[256,1408]{1,0:T(8,128)(2,1)S(1)}, bf16[256,1408]{1,0:T(8,128)(2,1)S(1)}, u32[]{:S(2)}, u32[]{:S(2)}) %collective-permute-start.36) | collective-permute-done | bytes 720928 | tf_op jit(solution)/shard_map/ppermute | solution.py:102
  167.1 14.8 %collective-permute-start.52 = (bf16[256,2048]{1,0:T(8,128)(2,1)}, bf16[256,2048]{1,0:T(8,128)(2,1)}, u32[]{:S(2)}, u32[]{:S(2)}) collective-permute-start(bf16[256,2048]{1,0:T(8,128)(2,1)} %collective-permute-done.51), channel_id=1, source_target_pairs={{0,1},{1,2},{2,3},{3,0},{4,5},{5,6},{6,7},{7,4},{8,9},{9,10},{10,1... | collective-permute-start | bytes 3145736 | tf_op jit(solution)/shard_map/ppermute | solution.py:108
  195.0 10.4 %fusion.144 = (f32[2,8,256]{2,1,0:T(8,128)}, f32[2,8,256,768]{2,3,1,0:T(8,128)}) fusion(pred[256,768]{0,1:T(8,128)(4,1)} %fusion.85, bf16[768,2,128,1]{0,2,3,1:T(8,128)(2,1)S(1)} %copy-done.88, bf16[256,2,8,128]{3,0,2,1:T(8,128)(2,1)} %bitcast.160), kind=kOutput, calls=%fused_computation.794 | convolution fusion | flops 817890048 | bytes 14237696 | tf_op jit(solution)/shard_map/sub | solution.py:211
  205.5 8.6 fusion.121
  214.1 9.0 copy.51
  245.4 7.4 collective-permute-done.46
  269.2 13.0 %collective-permute-done.40 = bf16[256,1408]{1,0:T(8,128)(2,1)S(1)} collective-permute-done((bf16[256,1408]{1,0:T(8,128)(2,1)S(1)}, bf16[256,1408]{1,0:T(8,128)(2,1)S(1)}, u32[]{:S(2)}, u32[]{:S(2)}) %collective-permute-start.40) | collective-permute-done | bytes 720928 | tf_op jit(solution)/shard_map/ppermute | solution.py:102
  338.0 13.6 %collective-permute-done.55 = bf16[256,2048]{1,0:T(8,128)(2,1)S(1)} collective-permute-done((bf16[256,2048]{1,0:T(8,128)(2,1)S(1)}, bf16[256,2048]{1,0:T(8,128)(2,1)S(1)}, u32[]{:S(2)}, u32[]{:S(2)}) %collective-permute-start.55) | collective-permute-done | bytes 1048608 | tf_op jit(solution)/shard_map/ppermute | solution.py:108
  361.4 12.6 %collective-permute-done.57 = bf16[256,2048]{1,0:T(8,128)(2,1)S(1)} collective-permute-done((bf16[256,2048]{1,0:T(8,128)(2,1)S(1)}, bf16[256,2048]{1,0:T(8,128)(2,1)S(1)}, u32[]{:S(2)}, u32[]{:S(2)}) %collective-permute-start.57) | collective-permute-done | bytes 1048608 | tf_op jit(solution)/shard_map/ppermute | solution.py:108
  379.1 17.4 %collective-permute-done.56 = bf16[256,2048]{1,0:T(8,128)(2,1)S(1)} collective-permute-done((bf16[256,2048]{1,0:T(8,128)(2,1)S(1)}, bf16[256,2048]{1,0:T(8,128)(2,1)S(1)}, u32[]{:S(2)}, u32[]{:S(2)}) %collective-permute-start.56) | collective-permute-done | bytes 1048608 | tf_op jit(solution)/shard_map/ppermute | solution.py:108
  406.4 11.4 %collective-permute-done.58 = bf16[256,2048]{1,0:T(8,128)(2,1)S(1)} collective-permute-done((bf16[256,2048]{1,0:T(8,128)(2,1)S(1)}, bf16[256,2048]{1,0:T(8,128)(2,1)S(1)}, u32[]{:S(2)}, u32[]{:S(2)}) %collective-permute-start.58) | collective-permute-done | bytes 1048608 | tf_op jit(solution)/shard_map/ppermute | solution.py:108
  423.4 8.3 convolution_convert_fusion.2
  442.0 8.3 convolution_convert_fusion.1
  461.2 8.1 convolution_convert_fusion
  484.1 6.8 fusion.63
  517.5 7.2 fusion.66
  587.5 37.9 %psum.7 = f32[2,2048]{1,0:T(2,128)S(1)} all-reduce(f32[2,2048]{1,0:T(2,128)S(1)} %constant_dynamic-update-slice_fusion.67), channel_id=1, replica_groups=mesh['dp'=2,'rows'=4,'cols'=4] {'dp','rows','cols'}, use_global_device_ids=true, to_apply=%region_9.10 | all-reduce | flops 4096 | bytes 32768 | tf_op jit(solution)/shard_map/psum | solution.py:330
  640.7 9.6 %collective-permute-done.106 = bf16[704,512]{1,0:T(8,128)(2,1)S(1)} collective-permute-done((bf16[704,512]{1,0:T(8,128)(2,1)S(1)}, bf16[704,512]{1,0:T(8,128)(2,1)S(1)}, u32[]{:S(2)}, u32[]{:S(2)}) %collective-permute-start.106) | collective-permute-done | bytes 720928 | tf_op jit(solution)/shard_map/ppermute | solution.py:102
  656.7 7.0 collective-permute-done.107
  675.8 6.6 convert_add_fusion
  720.2 18.8 %collective-permute-done.79 = bf16[256,512]{1,0:T(8,128)(2,1)} collective-permute-done((bf16[256,512]{1,0:T(8,128)(2,1)}, bf16[256,512]{1,0:T(8,128)(2,1)}, u32[]{:S(2)}, u32[]{:S(2)}) %collective-permute-start.79) | collective-permute-done | bytes 262176 | tf_op jit(solution)/shard_map/ppermute | solution.py:114
  740.4 12.2 %collective-permute-done.78 = bf16[256,512]{1,0:T(8,128)(2,1)S(1)} collective-permute-done((bf16[256,512]{1,0:T(8,128)(2,1)}, bf16[256,512]{1,0:T(8,128)(2,1)S(1)}, u32[]{:S(2)}, u32[]{:S(2)}) %collective-permute-start.78) | collective-permute-done | bytes 262176 | tf_op jit(solution)/shard_map/ppermute | solution.py:114
  766.6 17.7 %collective-permute-done.88 = bf16[1024,512]{0,1:T(8,128)(2,1)S(1)} collective-permute-done((bf16[1024,512]{0,1:T(8,128)(2,1)}, bf16[1024,512]{0,1:T(8,128)(2,1)S(1)}, u32[]{:S(2)}, u32[]{:S(2)}) %collective-permute-start.88) | collective-permute-done | bytes 1048608 | tf_op jit(solution)/shard_map/ppermute | solution.py:102
  786.4 18.6 %collective-permute-done.80 = bf16[256,512]{1,0:T(8,128)(2,1)S(1)} collective-permute-done((bf16[256,512]{1,0:T(8,128)(2,1)S(1)}, bf16[256,512]{1,0:T(8,128)(2,1)S(1)}, u32[]{:S(2)}, u32[]{:S(2)}) %collective-permute-start.80) | collective-permute-done | bytes 262176 | tf_op jit(solution)/shard_map/ppermute | solution.py:102
  825.2 23.8 %collective-permute-done.100 = bf16[512,1408]{1,0:T(8,128)(2,1)S(1)} collective-permute-done((bf16[512,1408]{1,0:T(8,128)(2,1)S(1)}, bf16[512,1408]{1,0:T(8,128)(2,1)S(1)}, u32[]{:S(2)}, u32[]{:S(2)}) %collective-permute-start.100) | collective-permute-done | bytes 1441824 | tf_op jit(solution)/shard_map/ppermute | solution.py:102
  852.1 8.1 collective-permute-done.70
  861.0 10.4 %collective-permute-done.92 = bf16[1024,256]{0,1:T(8,128)(2,1)S(1)} collective-permute-done((bf16[1024,256]{0,1:T(8,128)(2,1)S(1)}, bf16[1024,256]{0,1:T(8,128)(2,1)S(1)}, u32[]{:S(2)}, u32[]{:S(2)}) %collective-permute-start.92) | collective-permute-done | bytes 524320 | tf_op jit(solution)/shard_map/ppermute | solution.py:102
  873.0 17.0 %collective-permute-done.72 = bf16[256,512]{1,0:T(8,128)(2,1)S(1)} collective-permute-done((bf16[256,512]{1,0:T(8,128)(2,1)S(1)}, bf16[256,512]{1,0:T(8,128)(2,1)S(1)}, u32[]{:S(2)}, u32[]{:S(2)}) %collective-permute-start.72) | collective-permute-done | bytes 262176 | tf_op jit(solution)/shard_map/ppermute | solution.py:114
  896.2 8.1 collective-permute-done.94
  (875 shorter events, 509.2 us)
Async XLA Ops:
  39.7 38.0 %collective-permute-start.13 = (bf16[128,2048]{1,0:T(8,128)(2,1)}, bf16[128,2048]{1,0:T(8,128)(2,1)}, u32[]{:S(2)}, u32[]{:S(2)}) collective-permute-start(bf16[128,2048]{1,0:T(8,128)(2,1)} %get-tuple-element.23), channel_id=1, source_target_pairs={{0,4},{4,0},{8,12},{12,8},{1,5},{5,1},{9,13},{13,9},{2,6},{6,2},{1... | collective-permute-start | bytes 1572872 | tf_op jit(solution)/shard_map/ppermute | solution.py:102
  51.7 52.9 %collective-permute-start.11 = (bf16[256,2048]{1,0:T(8,128)(2,1)}, bf16[256,2048]{1,0:T(8,128)(2,1)}, u32[]{:S(2)}, u32[]{:S(2)}) collective-permute-start(bf16[256,2048]{1,0:T(8,128)(2,1)} %pad_maximum_fusion.13), channel_id=1, source_target_pairs={{0,16},{16,0},{1,17},{17,1},{2,18},{18,2},{3,19},{19,3},{4,20},{20... | collective-permute-start | bytes 3145736 | tf_op jit(solution)/shard_map/ppermute | solution.py:105
  84.3 72.8 %collective-permute-start.51 = (bf16[256,2048]{1,0:T(8,128)(2,1)}, bf16[256,2048]{1,0:T(8,128)(2,1)}, u32[]{:S(2)}, u32[]{:S(2)}) collective-permute-start(bf16[256,2048]{1,0:T(8,128)(2,1)} %multiply_convert_fusion.1), channel_id=1, source_target_pairs={{0,1},{1,2},{2,3},{3,0},{4,5},{5,6},{6,7},{7,4},{8,9},{9,10},{10,1... | collective-permute-start | bytes 3145736 | tf_op jit(solution)/shard_map/ppermute | solution.py:108
  152.3 105.4 %collective-permute-start.32 = (bf16[256,1408]{1,0:T(8,128)(2,1)}, bf16[256,1408]{1,0:T(8,128)(2,1)}, u32[]{:S(2)}, u32[]{:S(2)}) collective-permute-start(bf16[256,1408]{1,0:T(8,128)(2,1)} %get-tuple-element.25), channel_id=1, source_target_pairs={{0,8},{4,12},{8,0},{12,4},{1,9},{5,13},{9,1},{13,5},{2,10},{6,14},... | collective-permute-start | bytes 2162696 | tf_op jit(solution)/shard_map/ppermute | solution.py:102
  154.7 68.4 %collective-permute-start.23 = (bf16[2048,256]{1,0:T(8,128)(2,1)}, bf16[2048,256]{1,0:T(8,128)(2,1)}, u32[]{:S(2)}, u32[]{:S(2)}) collective-permute-start(bf16[2048,256]{1,0:T(8,128)(2,1)} %pad_maximum_fusion.18), channel_id=1, source_target_pairs={{0,16},{16,0},{1,17},{17,1},{2,18},{18,2},{3,19},{19,3},{4,20},{20... | collective-permute-start | bytes 3145736 | tf_op jit(solution)/shard_map/ppermute | solution.py:105
  157.1 76.4 %collective-permute-start.26 = (bf16[2048,256]{1,0:T(8,128)(2,1)}, bf16[2048,256]{1,0:T(8,128)(2,1)}, u32[]{:S(2)}, u32[]{:S(2)}) collective-permute-start(bf16[2048,256]{1,0:T(8,128)(2,1)} %pad_maximum_fusion.19), channel_id=1, source_target_pairs={{0,16},{16,0},{1,17},{17,1},{2,18},{18,2},{3,19},{19,3},{4,20},{20... | collective-permute-start | bytes 3145736 | tf_op jit(solution)/shard_map/ppermute | solution.py:105
  167.1 100.5 %collective-permute-start.52 = (bf16[256,2048]{1,0:T(8,128)(2,1)}, bf16[256,2048]{1,0:T(8,128)(2,1)}, u32[]{:S(2)}, u32[]{:S(2)}) collective-permute-start(bf16[256,2048]{1,0:T(8,128)(2,1)} %collective-permute-done.51), channel_id=1, source_target_pairs={{0,1},{1,2},{2,3},{3,0},{4,5},{5,6},{6,7},{7,4},{8,9},{9,10},{10,1... | collective-permute-start | bytes 3145736 | tf_op jit(solution)/shard_map/ppermute | solution.py:108
  184.6 56.2 %collective-permute-start.42 = (bf16[704,256]{1,0:T(8,128)(2,1)}, bf16[704,256]{1,0:T(8,128)(2,1)}, u32[]{:S(2)}, u32[]{:S(2)}) collective-permute-start(bf16[704,256]{1,0:T(8,128)(2,1)} %get-tuple-element.388), channel_id=1, source_target_pairs={{0,4},{4,0},{8,12},{12,8},{1,5},{5,1},{9,13},{13,9},{2,6},{6,2},{1... | collective-permute-start | bytes 1081352 | tf_op jit(solution)/shard_map/ppermute | solution.py:102
  268.2 51.9 %collective-permute-start.53 = (bf16[256,2048]{1,0:T(8,128)(2,1)}, bf16[256,2048]{1,0:T(8,128)(2,1)S(1)}, u32[]{:S(2)}, u32[]{:S(2)}) collective-permute-start(bf16[256,2048]{1,0:T(8,128)(2,1)} %collective-permute-done.52), channel_id=1, source_target_pairs={{0,1},{1,2},{2,3},{3,0},{4,5},{5,6},{6,7},{7,4},{8,9},{9,10},{10,1... | collective-permute-start | bytes 3145736 | tf_op jit(solution)/shard_map/ppermute | solution.py:108
  351.6 44.9 %collective-permute-start.56 = (bf16[256,2048]{1,0:T(8,128)(2,1)S(1)}, bf16[256,2048]{1,0:T(8,128)(2,1)S(1)}, u32[]{:S(2)}, u32[]{:S(2)}) collective-permute-start(bf16[256,2048]{1,0:T(8,128)(2,1)S(1)} %collective-permute-done.55), channel_id=1, source_target_pairs={{0,1},{1,2},{2,3},{3,0},{4,5},{5,6},{6,7},{7,4},{8,9},{9,10},{10,1... | collective-permute-start | bytes 3145736 | tf_op jit(solution)/shard_map/ppermute | solution.py:108
  378.6 39.1 %collective-permute-start.58 = (bf16[256,2048]{1,0:T(8,128)(2,1)S(1)}, bf16[256,2048]{1,0:T(8,128)(2,1)S(1)}, u32[]{:S(2)}, u32[]{:S(2)}) collective-permute-start(bf16[256,2048]{1,0:T(8,128)(2,1)S(1)} %fusion.45), channel_id=1, source_target_pairs={{0,1},{1,2},{2,3},{3,0},{4,5},{5,6},{6,7},{7,4},{8,9},{9,10},{10,1... | collective-permute-start | bytes 3145736 | tf_op jit(solution)/shard_map/ppermute | solution.py:108
  423.4 54.4 %collective-permute-start.59 = (bf16[256,2048]{1,0:T(8,128)(2,1)}, bf16[256,2048]{1,0:T(8,128)(2,1)S(1)}, u32[]{:S(2)}, u32[]{:S(2)}) collective-permute-start(bf16[256,2048]{1,0:T(8,128)(2,1)} %fusion.46), channel_id=1, source_target_pairs={{0,1},{1,2},{2,3},{3,0},{4,5},{5,6},{6,7},{7,4},{8,9},{9,10},{10,1... | collective-permute-start | bytes 3145736 | tf_op jit(solution)/shard_map/ppermute | solution.py:108
  442.0 223.9 %collective-permute-start.96 = (bf16[1024,1408]{1,0:T(8,128)(2,1)}, bf16[1024,1408]{1,0:T(8,128)(2,1)}, u32[]{:S(2)}, u32[]{:S(2)}) collective-permute-start(bf16[1024,1408]{1,0:T(8,128)(2,1)} %pad_maximum_fusion.1), channel_id=1, source_target_pairs={{0,16},{16,0},{1,17},{17,1},{2,18},{18,2},{3,19},{19,3},{4,20},{20... | collective-permute-start | bytes 8650760 | tf_op jit(solution)/shard_map/ppermute | solution.py:105
  460.6 213.9 %collective-permute-start.99 = (bf16[1024,1408]{1,0:T(8,128)(2,1)}, bf16[1024,1408]{1,0:T(8,128)(2,1)}, u32[]{:S(2)}, u32[]{:S(2)}) collective-permute-start(bf16[1024,1408]{1,0:T(8,128)(2,1)} %pad_maximum_fusion.2), channel_id=1, source_target_pairs={{0,16},{16,0},{1,17},{17,1},{2,18},{18,2},{3,19},{19,3},{4,20},{20... | collective-permute-start | bytes 8650760 | tf_op jit(solution)/shard_map/ppermute | solution.py:105
  473.5 155.4 %collective-permute-start.105 = (bf16[704,1024]{1,0:T(8,128)(2,1)}, bf16[704,1024]{1,0:T(8,128)(2,1)}, u32[]{:S(2)}, u32[]{:S(2)}) collective-permute-start(bf16[704,1024]{1,0:T(8,128)(2,1)} %pad_maximum_fusion.10), channel_id=1, source_target_pairs={{0,16},{16,0},{1,17},{17,1},{2,18},{18,2},{3,19},{19,3},{4,20},{20... | collective-permute-start | bytes 4325384 | tf_op jit(solution)/shard_map/ppermute | solution.py:105
  565.8 65.3 %collective-permute-start.102 = (bf16[704,1024]{1,0:T(8,128)(2,1)}, bf16[704,1024]{1,0:T(8,128)(2,1)}, u32[]{:S(2)}, u32[]{:S(2)}) collective-permute-start(bf16[704,1024]{1,0:T(8,128)(2,1)} %pad_maximum_fusion.9), channel_id=1, source_target_pairs={{0,16},{16,0},{1,17},{17,1},{2,18},{18,2},{3,19},{19,3},{4,20},{20... | collective-permute-start | bytes 4325384 | tf_op jit(solution)/shard_map/ppermute | solution.py:105
  566.3 69.5 %collective-permute-start.60 = (bf16[256,2048]{1,0:T(8,128)(2,1)}, bf16[256,2048]{1,0:T(8,128)(2,1)}, u32[]{:S(2)}, u32[]{:S(2)}) collective-permute-start(bf16[256,2048]{1,0:T(8,128)(2,1)} %convolution_convert_fusion.7), channel_id=1, source_target_pairs={{0,1},{1,2},{2,3},{3,0},{4,5},{5,6},{6,7},{7,4},{8,9},{9,10},{10,1... | collective-permute-start | bytes 3145736 | tf_op jit(solution)/shard_map/ppermute | solution.py:108
  650.3 50.4 %collective-permute-start.65 = (bf16[1024,1024]{1,0:T(8,128)(2,1)}, bf16[1024,1024]{1,0:T(8,128)(2,1)}, u32[]{:S(2)}, u32[]{:S(2)}) collective-permute-start(bf16[1024,1024]{1,0:T(8,128)(2,1)} %pad_maximum_fusion.3), channel_id=1, source_target_pairs={{0,16},{16,0},{1,17},{17,1},{2,18},{18,2},{3,19},{19,3},{4,20},{20... | collective-permute-start | bytes 6291464 | tf_op jit(solution)/shard_map/ppermute | solution.py:105
  663.7 49.7 %collective-permute-start.68 = (bf16[1024,1024]{1,0:T(8,128)(2,1)}, bf16[1024,1024]{1,0:T(8,128)(2,1)}, u32[]{:S(2)}, u32[]{:S(2)}) collective-permute-start(bf16[1024,1024]{1,0:T(8,128)(2,1)} %pad_maximum_fusion.4), channel_id=1, source_target_pairs={{0,16},{16,0},{1,17},{17,1},{2,18},{18,2},{3,19},{19,3},{4,20},{20... | collective-permute-start | bytes 6291464 | tf_op jit(solution)/shard_map/ppermute | solution.py:105
  664.3 41.9 %collective-permute-start.87 = (bf16[1024,1024]{0,1:T(8,128)(2,1)}, bf16[1024,1024]{0,1:T(8,128)(2,1)}, u32[]{:S(2)}, u32[]{:S(2)}) collective-permute-start(bf16[1024,1024]{0,1:T(8,128)(2,1)} %pad_maximum_fusion.5), channel_id=1, source_target_pairs={{0,16},{16,0},{1,17},{17,1},{2,18},{18,2},{3,19},{19,3},{4,20},{20... | collective-permute-start | bytes 6291464 | tf_op jit(solution)/shard_map/ppermute | solution.py:105
  700.7 121.7 %collective-permute-start.97 = (bf16[512,1408]{1,0:T(8,128)(2,1)S(1)}, bf16[512,1408]{1,0:T(8,128)(2,1)}, u32[]{:S(2)}, u32[]{:S(2)}) collective-permute-start(bf16[512,1408]{1,0:T(8,128)(2,1)S(1)} %pad_maximum_fusion.8), channel_id=1, source_target_pairs={{0,4},{4,0},{8,12},{12,8},{1,5},{5,1},{9,13},{13,9},{2,6},{6,2},{1... | collective-permute-start | bytes 4325384 | tf_op jit(solution)/shard_map/ppermute | solution.py:102
  705.1 50.6 %collective-permute-start.62 = (bf16[256,2048]{1,0:T(8,128)(2,1)}, bf16[256,2048]{1,0:T(8,128)(2,1)}, u32[]{:S(2)}, u32[]{:S(2)}) collective-permute-start(bf16[256,2048]{1,0:T(8,128)(2,1)} %fusion.42), channel_id=1, source_target_pairs={{0,1},{1,2},{2,3},{3,0},{4,5},{5,6},{6,7},{7,4},{8,9},{9,10},{10,1... | collective-permute-start | bytes 3145736 | tf_op jit(solution)/shard_map/ppermute | solution.py:108
  713.5 39.2 %collective-permute-start.78 = (bf16[256,512]{1,0:T(8,128)(2,1)}, bf16[256,512]{1,0:T(8,128)(2,1)S(1)}, u32[]{:S(2)}, u32[]{:S(2)}) collective-permute-start(bf16[256,512]{1,0:T(8,128)(2,1)} %fusion.95), channel_id=1, source_target_pairs={{0,2},{1,3},{2,0},{3,1},{4,6},{5,7},{6,4},{7,5},{8,10},{9,11},{10,... | collective-permute-start | bytes 786440 | tf_op jit(solution)/shard_map/ppermute | solution.py:114
  716.7 37.5 %collective-permute-start.77 = (bf16[256,512]{1,0:T(8,128)(2,1)}, bf16[256,512]{1,0:T(8,128)(2,1)S(1)}, u32[]{:S(2)}, u32[]{:S(2)}) collective-permute-start(bf16[256,512]{1,0:T(8,128)(2,1)} %fusion.95), channel_id=1, source_target_pairs={{0,1},{1,0},{2,3},{3,2},{4,5},{5,4},{6,7},{7,6},{8,9},{9,8},{10,11... | collective-permute-start | bytes 786440 | tf_op jit(solution)/shard_map/ppermute | solution.py:114
  752.7 52.3 %collective-permute-start.69 = (bf16[512,1024]{1,0:T(8,128)(2,1)}, bf16[512,1024]{1,0:T(8,128)(2,1)S(1)}, u32[]{:S(2)}, u32[]{:S(2)}) collective-permute-start(bf16[512,1024]{1,0:T(8,128)(2,1)} %pad_maximum_fusion.22), channel_id=1, source_target_pairs={{0,4},{4,0},{8,12},{12,8},{1,5},{5,1},{9,13},{13,9},{2,6},{6,2},{1... | collective-permute-start | bytes 3145736 | tf_op jit(solution)/shard_map/ppermute | solution.py:102
  755.7 58.0 %collective-permute-start.91 = (bf16[1024,512]{0,1:T(8,128)(2,1)}, bf16[1024,512]{0,1:T(8,128)(2,1)S(1)}, u32[]{:S(2)}, u32[]{:S(2)}) collective-permute-start(bf16[1024,512]{0,1:T(8,128)(2,1)} %pad_maximum_fusion.24), channel_id=1, source_target_pairs={{0,4},{4,0},{8,12},{12,8},{1,5},{5,1},{9,13},{13,9},{2,6},{6,2},{1... | collective-permute-start | bytes 3145736 | tf_op jit(solution)/shard_map/ppermute | solution.py:102
  764.7 40.3 %collective-permute-start.80 = (bf16[256,512]{1,0:T(8,128)(2,1)S(1)}, bf16[256,512]{1,0:T(8,128)(2,1)S(1)}, u32[]{:S(2)}, u32[]{:S(2)}) collective-permute-start(bf16[256,512]{1,0:T(8,128)(2,1)S(1)} %add_convert_fusion.2), channel_id=1, source_target_pairs={{0,4},{4,0},{8,12},{12,8},{1,5},{5,1},{9,13},{13,9},{2,6},{6,2},{1... | collective-permute-start | bytes 786440 | tf_op jit(solution)/shard_map/ppermute | solution.py:102
  816.4 43.8 %collective-permute-start.70 = (bf16[256,1024]{1,0:T(8,128)(2,1)}, bf16[256,1024]{1,0:T(8,128)(2,1)S(1)}, u32[]{:S(2)}, u32[]{:S(2)}) collective-permute-start(bf16[256,1024]{1,0:T(8,128)(2,1)} %fusion.74), channel_id=1, source_target_pairs={{0,8},{4,12},{8,0},{12,4},{1,9},{5,13},{9,1},{13,5},{2,10},{6,14},... | collective-permute-start | bytes 1572872 | tf_op jit(solution)/shard_map/ppermute | solution.py:102
  818.0 42.6 %collective-permute-start.89 = (bf16[1024,256]{0,1:T(8,128)(2,1)S(1)}, bf16[1024,256]{0,1:T(8,128)(2,1)S(1)}, u32[]{:S(2)}, u32[]{:S(2)}) collective-permute-start(bf16[1024,256]{0,1:T(8,128)(2,1)S(1)} %fusion.71), channel_id=1, source_target_pairs={{0,4},{4,0},{8,12},{12,8},{1,5},{5,1},{9,13},{13,9},{2,6},{6,2},{1... | collective-permute-start | bytes 1572872 | tf_op jit(solution)/shard_map/ppermute | solution.py:102
  822.4 49.0 %collective-permute-start.92 = (bf16[1024,256]{0,1:T(8,128)(2,1)S(1)}, bf16[1024,256]{0,1:T(8,128)(2,1)S(1)}, u32[]{:S(2)}, u32[]{:S(2)}) collective-permute-start(bf16[1024,256]{0,1:T(8,128)(2,1)S(1)} %fusion.68), channel_id=1, source_target_pairs={{0,8},{4,12},{8,0},{12,4},{1,9},{5,13},{9,1},{13,5},{2,10},{6,14},... | collective-permute-start | bytes 1572872 | tf_op jit(solution)/shard_map/ppermute | solution.py:102
  848.9 56.6 %collective-permute-start.98 = (bf16[256,1408]{1,0:T(8,128)(2,1)S(1)}, bf16[256,1408]{1,0:T(8,128)(2,1)S(1)}, u32[]{:S(2)}, u32[]{:S(2)}) collective-permute-start(bf16[256,1408]{1,0:T(8,128)(2,1)S(1)} %fusion.59), channel_id=1, source_target_pairs={{0,8},{4,12},{8,0},{12,4},{1,9},{5,13},{9,1},{13,5},{2,10},{6,14},... | collective-permute-start | bytes 2162696 | tf_op jit(solution)/shard_map/ppermute | solution.py:102
  851.5 56.9 %collective-permute-start.101 = (bf16[256,1408]{1,0:T(8,128)(2,1)}, bf16[256,1408]{1,0:T(8,128)(2,1)}, u32[]{:S(2)}, u32[]{:S(2)}) collective-permute-start(bf16[256,1408]{1,0:T(8,128)(2,1)} %fusion.57), channel_id=1, source_target_pairs={{0,4},{4,0},{8,12},{12,8},{1,5},{5,1},{9,13},{13,9},{2,6},{6,2},{1... | collective-permute-start | bytes 2162696 | tf_op jit(solution)/shard_map/ppermute | solution.py:102
  (255 other events, 4046.8 us)
where the time goes:
time: 922 us; the launch traced here: 911 us
  waiting for transfers between devices  318 us (34%)
  matrix products  175 us (19%)
  other arithmetic  159 us (17%)
  local copies, waits for them, and re-layouts  110 us (12%)
  starting transfers between devices  107 us (12%)
  blocking collectives  37.9 us (4%)
    ppermute x48, waiting for transfers between devices, to_rows(): return lax.ppermute(value, 'rows', [(i, i ^ a) for i in range(rows)])  192 us
    dot_general x36, matrix products, dot(): lax.dot_general(left, right, ((dims[:1], dims[1:]), ((), ())), preferred_...  150 us
    unnamed x413, local copies, waits for them, and re-layouts  75.2 us
    ppermute x12, waiting for transfers between devices, to_xor_cols(): return lax.ppermute(value, 'cols', [(i, i ^ k) for i in range(cols)])  65.2 us
    ppermute x12, waiting for transfers between devices, to_cols(): lax.ppermute(value, 'cols', [(i, (i + k) % cols) for i in range(cols)])  60.6 us
    ppermute x48, starting transfers between devices, to_rows(): return lax.ppermute(value, 'rows', [(i, i ^ a) for i in range(rows)])  55 us
    psum x1, blocking collectives, local(): gains = lax.psum(xor_order(gains, place, blocks, 1), ('dp', 'rows', 'cols'))  37.9 us
    select_n x30, other arithmetic, xor_blocks(): jnp.where(swap, blocks[j ^ bit], blocks[j])  34.6 us
  transfers between devices with their start and end apart: 108, of which 36 were waited for; matrix products, arithmetic and copies ran while one was open for 46% of the time, Pallas kernels for 0%

commit v1 on v0

--- a/solution.py
+++ b/solution.py
@@ -327,7 +327,9 @@
     found = jnp.concatenate(xor_blocks(found, d * rows + r), 0).astype(f32)
     key_grad, value_grad = (found[:, :kv_width], found[:, kv_width:])
     gains = jnp.stack([attention_gain_part, mlp_gain_part])
-    gains = lax.psum(xor_order(gains, place, blocks, 1), ("dp", "rows", "cols"))
+    gains = jnp.sum(
+        lax.all_gather(xor_order(gains, place, blocks, 1), ("dp", "rows", "cols")), axis=0
+    )
     return (
         xor_order(output, place, blocks, 1),
         input_grad,

time: 922 us -> 964 us (1.046)
  blocking collectives: 37.9 us -> 77.4 us
    all_gather x0 -> x1, blocking collectives: none -> 77.4 us  [local(): lax.all_gather(xor_order(gains, place, blocks, 1), ('dp', 'rows', 'cols'))]
    psum x1 -> x0, blocking collectives: 37.9 us -> none  [local(): gains = lax.psum(xor_order(gains, place, blocks, 1), ('dp', 'rows', 'cols'))]
    unnamed x413 -> x421, local copies, waits for them, and re-layouts: 75.2 us -> 73.3 us
  transfers between devices with their start and end apart: 108 -> 108, of which waited for: 36 -> 37; matrix products, arithmetic and copies ran while one was open for 46% -> 44% of each run, Pallas kernels for 0% -> 0%
where the time goes in v1:
time: 964 us; the launch traced here: 954 us
  waiting for transfers between devices  321 us (33%)
  matrix products  175 us (18%)
  other arithmetic  163 us (17%)
  starting transfers between devices  107 us (11%)
  local copies, waits for them, and re-layouts  106 us (11%)
  blocking collectives  77.4 us (8%)
    ppermute x48, waiting for transfers between devices, to_rows(): return lax.ppermute(value, 'rows', [(i, i ^ a) for i in range(rows)])  195 us
    dot_general x36, matrix products, dot(): lax.dot_general(left, right, ((dims[:1], dims[1:]), ((), ())), preferred_...  151 us
    all_gather x1, blocking collectives, local(): lax.all_gather(xor_order(gains, place, blocks, 1), ('dp', 'rows', 'cols'))  77.4 us
    unnamed x421, local copies, waits for them, and re-layouts  73.3 us
    ppermute x12, waiting for transfers between devices, to_cols(): lax.ppermute(value, 'cols', [(i, (i + k) % cols) for i in range(cols)])  63.4 us
    ppermute x12, waiting for transfers between devices, to_xor_cols(): return lax.ppermute(value, 'cols', [(i, i ^ k) for i in range(cols)])  62.2 us
    ppermute x48, starting transfers between devices, to_rows(): return lax.ppermute(value, 'rows', [(i, i ^ a) for i in range(rows)])  56 us
    select_n x30, other arithmetic, xor_blocks(): jnp.where(swap, blocks[j ^ bit], blocks[j])  34.5 us
  transfers between devices with their start and end apart: 108, of which 37 were waited for; matrix products, arithmetic and copies ran while one was open for 44% of the time, Pallas kernels for 0%

profile of v1, /device:TPU:0, one launch (start us, length us, event | category | flops | bytes accessed | tf_op | source)
XLA Modules:
  0.0 953.6 jit_solution(8140685641167398144)
XLA Ops:
  58.5 12.0 %collective-permute-done.16 = bf16[128,2048]{1,0:T(8,128)(2,1)} collective-permute-done((bf16[128,2048]{1,0:T(8,128)(2,1)S(1)}, bf16[128,2048]{1,0:T(8,128)(2,1)}, u32[]{:S(2)}, u32[]{:S(2)}) %collective-permute-start.16) | collective-permute-done | bytes 524320 | tf_op jit(solution)/shard_map/ppermute | solution.py:102
  138.2 11.1 %collective-permute-done.28 = bf16[1024,256]{1,0:T(8,128)(2,1)S(1)} collective-permute-done((bf16[1024,256]{1,0:T(8,128)(2,1)S(1)}, bf16[1024,256]{1,0:T(8,128)(2,1)S(1)}, u32[]{:S(2)}, u32[]{:S(2)}) %collective-permute-start.28) | collective-permute-done | bytes 524320 | tf_op jit(solution)/shard_map/ppermute | solution.py:102
  155.4 8.8 collective-permute-done.36
  164.2 14.9 %collective-permute-start.52 = (bf16[256,2048]{1,0:T(8,128)(2,1)}, bf16[256,2048]{1,0:T(8,128)(2,1)}, u32[]{:S(2)}, u32[]{:S(2)}) collective-permute-start(bf16[256,2048]{1,0:T(8,128)(2,1)} %collective-permute-done.51), channel_id=1, source_target_pairs={{0,1},{1,2},{2,3},{3,0},{4,5},{5,6},{6,7},{7,4},{8,9},{9,10},{10,1... | collective-permute-start | bytes 3145736 | tf_op jit(solution)/shard_map/ppermute | solution.py:108
  192.7 10.0 %fusion.144 = (f32[2,8,256]{2,1,0:T(8,128)S(1)}, f32[2,8,256,768]{2,3,1,0:T(8,128)}) fusion(pred[256,768]{0,1:T(8,128)(4,1)S(1)} %copy-done.134, bf16[768,2,128,1]{0,2,3,1:T(8,128)(2,1)S(1)} %copy-done.97, bf16[256,2,8,128]{3,0,2,1:T(8,128)(2,1)} %bitcast.161), kind=kOutput, calls=%fused_computation.794 | convolution fusion | flops 817890048 | bytes 14237696 | tf_op jit(solution)/shard_map/sub | solution.py:211
  202.7 8.4 fusion.121
  211.1 9.1 copy.68
  241.0 8.2 collective-permute-done.46
  265.5 12.3 %collective-permute-done.40 = bf16[256,1408]{1,0:T(8,128)(2,1)S(1)} collective-permute-done((bf16[256,1408]{1,0:T(8,128)(2,1)S(1)}, bf16[256,1408]{1,0:T(8,128)(2,1)S(1)}, u32[]{:S(2)}, u32[]{:S(2)}) %collective-permute-start.40) | collective-permute-done | bytes 720928 | tf_op jit(solution)/shard_map/ppermute | solution.py:102
  333.6 13.6 %collective-permute-done.55 = bf16[256,2048]{1,0:T(8,128)(2,1)S(1)} collective-permute-done((bf16[256,2048]{1,0:T(8,128)(2,1)S(1)}, bf16[256,2048]{1,0:T(8,128)(2,1)S(1)}, u32[]{:S(2)}, u32[]{:S(2)}) %collective-permute-start.55) | collective-permute-done | bytes 1048608 | tf_op jit(solution)/shard_map/ppermute | solution.py:108
  357.1 12.6 %collective-permute-done.57 = bf16[256,2048]{1,0:T(8,128)(2,1)S(1)} collective-permute-done((bf16[256,2048]{1,0:T(8,128)(2,1)S(1)}, bf16[256,2048]{1,0:T(8,128)(2,1)S(1)}, u32[]{:S(2)}, u32[]{:S(2)}) %collective-permute-start.57) | collective-permute-done | bytes 1048608 | tf_op jit(solution)/shard_map/ppermute | solution.py:108
  374.6 17.5 %collective-permute-done.56 = bf16[256,2048]{1,0:T(8,128)(2,1)S(1)} collective-permute-done((bf16[256,2048]{1,0:T(8,128)(2,1)S(1)}, bf16[256,2048]{1,0:T(8,128)(2,1)S(1)}, u32[]{:S(2)}, u32[]{:S(2)}) %collective-permute-start.56) | collective-permute-done | bytes 1048608 | tf_op jit(solution)/shard_map/ppermute | solution.py:108
  402.1 11.2 %collective-permute-done.58 = bf16[256,2048]{1,0:T(8,128)(2,1)S(1)} collective-permute-done((bf16[256,2048]{1,0:T(8,128)(2,1)S(1)}, bf16[256,2048]{1,0:T(8,128)(2,1)S(1)}, u32[]{:S(2)}, u32[]{:S(2)}) %collective-permute-start.58) | collective-permute-done | bytes 1048608 | tf_op jit(solution)/shard_map/ppermute | solution.py:108
  418.8 8.8 convolution_convert_fusion.2
  437.8 9.2 convolution_convert_fusion.1
  457.8 8.7 convolution_convert_fusion
  481.0 6.8 fusion.63
  514.6 7.2 fusion.66
  584.6 77.4 %all-gather.1 = f32[32,2,2048]{2,1,0:T(2,128)} all-gather(f32[1,2,2048]{2,1,0:T(2,128)S(1)} %bitcast.176), channel_id=2, replica_groups=mesh['dp'=2,'rows'=4,'cols'=4] {'dp','rows','cols'}, dimensions={0}, use_global_device_ids=true | all-gather | bytes 540672 | tf_op jit(solution)/shard_map/all_gather | solution.py:331
  669.0 8.6 collective-permute-start.106
  684.9 9.5 collective-permute-done.106
  699.5 8.4 collective-permute-done.107
  717.9 6.6 convert_add_fusion
  763.9 19.2 %collective-permute-done.79 = bf16[256,512]{1,0:T(8,128)(2,1)S(1)} collective-permute-done((bf16[256,512]{1,0:T(8,128)(2,1)S(1)}, bf16[256,512]{1,0:T(8,128)(2,1)S(1)}, u32[]{:S(2)}, u32[]{:S(2)}) %collective-permute-start.79) | collective-permute-done | bytes 262176 | tf_op jit(solution)/shard_map/ppermute | solution.py:114
  784.5 9.8 %collective-permute-done.78 = bf16[256,512]{1,0:T(8,128)(2,1)S(1)} collective-permute-done((bf16[256,512]{1,0:T(8,128)(2,1)S(1)}, bf16[256,512]{1,0:T(8,128)(2,1)S(1)}, u32[]{:S(2)}, u32[]{:S(2)}) %collective-permute-start.78) | collective-permute-done | bytes 262176 | tf_op jit(solution)/shard_map/ppermute | solution.py:114
  810.7 18.3 %collective-permute-done.88 = bf16[1024,512]{0,1:T(8,128)(2,1)S(1)} collective-permute-done((bf16[1024,512]{0,1:T(8,128)(2,1)}, bf16[1024,512]{0,1:T(8,128)(2,1)S(1)}, u32[]{:S(2)}, u32[]{:S(2)}) %collective-permute-start.88) | collective-permute-done | bytes 1048608 | tf_op jit(solution)/shard_map/ppermute | solution.py:102
  830.4 15.3 %collective-permute-done.80 = bf16[256,512]{1,0:T(8,128)(2,1)S(1)} collective-permute-done((bf16[256,512]{1,0:T(8,128)(2,1)S(1)}, bf16[256,512]{1,0:T(8,128)(2,1)S(1)}, u32[]{:S(2)}, u32[]{:S(2)}) %collective-permute-start.80) | collective-permute-done | bytes 262176 | tf_op jit(solution)/shard_map/ppermute | solution.py:102
  866.6 23.9 %collective-permute-done.100 = bf16[512,1408]{1,0:T(8,128)(2,1)S(1)} collective-permute-done((bf16[512,1408]{1,0:T(8,128)(2,1)S(1)}, bf16[512,1408]{1,0:T(8,128)(2,1)S(1)}, u32[]{:S(2)}, u32[]{:S(2)}) %collective-permute-start.100) | collective-permute-done | bytes 1441824 | tf_op jit(solution)/shard_map/ppermute | solution.py:102
  893.6 8.2 collective-permute-done.70
  904.0 8.9 collective-permute-done.92
  915.0 19.1 %collective-permute-done.72 = bf16[256,512]{1,0:T(8,128)(2,1)S(1)} collective-permute-done((bf16[256,512]{1,0:T(8,128)(2,1)S(1)}, bf16[256,512]{1,0:T(8,128)(2,1)S(1)}, u32[]{:S(2)}, u32[]{:S(2)}) %collective-permute-start.72) | collective-permute-done | bytes 262176 | tf_op jit(solution)/shard_map/ppermute | solution.py:114
  938.5 7.7 collective-permute-done.94
  (884 shorter events, 517.8 us)
Async XLA Ops:
  37.5 37.9 %collective-permute-start.13 = (bf16[128,2048]{1,0:T(8,128)(2,1)S(1)}, bf16[128,2048]{1,0:T(8,128)(2,1)}, u32[]{:S(2)}, u32[]{:S(2)}) collective-permute-start(bf16[128,2048]{1,0:T(8,128)(2,1)S(1)} %get-tuple-element.23), channel_id=1, source_target_pairs={{0,4},{4,0},{8,12},{12,8},{1,5},{5,1},{9,13},{13,9},{2,6},{6,2},{1... | collective-permute-start | bytes 1572872 | tf_op jit(solution)/shard_map/ppermute | solution.py:102
  50.0 52.7 %collective-permute-start.11 = (bf16[256,2048]{1,0:T(8,128)(2,1)}, bf16[256,2048]{1,0:T(8,128)(2,1)}, u32[]{:S(2)}, u32[]{:S(2)}) collective-permute-start(bf16[256,2048]{1,0:T(8,128)(2,1)} %pad_maximum_fusion.13), channel_id=1, source_target_pairs={{0,16},{16,0},{1,17},{17,1},{2,18},{18,2},{3,19},{19,3},{4,20},{20... | collective-permute-start | bytes 3145736 | tf_op jit(solution)/shard_map/ppermute | solution.py:105
  81.1 74.1 %collective-permute-start.51 = (bf16[256,2048]{1,0:T(8,128)(2,1)}, bf16[256,2048]{1,0:T(8,128)(2,1)}, u32[]{:S(2)}, u32[]{:S(2)}) collective-permute-start(bf16[256,2048]{1,0:T(8,128)(2,1)} %multiply_convert_fusion.1), channel_id=1, source_target_pairs={{0,1},{1,2},{2,3},{3,0},{4,5},{5,6},{6,7},{7,4},{8,9},{9,10},{10,1... | collective-permute-start | bytes 3145736 | tf_op jit(solution)/shard_map/ppermute | solution.py:108
  149.3 104.6 %collective-permute-start.32 = (bf16[256,1408]{1,0:T(8,128)(2,1)}, bf16[256,1408]{1,0:T(8,128)(2,1)}, u32[]{:S(2)}, u32[]{:S(2)}) collective-permute-start(bf16[256,1408]{1,0:T(8,128)(2,1)} %get-tuple-element.25), channel_id=1, source_target_pairs={{0,8},{4,12},{8,0},{12,4},{1,9},{5,13},{9,1},{13,5},{2,10},{6,14},... | collective-permute-start | bytes 2162696 | tf_op jit(solution)/shard_map/ppermute | solution.py:102
  152.8 67.4 %collective-permute-start.23 = (bf16[2048,256]{1,0:T(8,128)(2,1)}, bf16[2048,256]{1,0:T(8,128)(2,1)}, u32[]{:S(2)}, u32[]{:S(2)}) collective-permute-start(bf16[2048,256]{1,0:T(8,128)(2,1)} %pad_maximum_fusion.18), channel_id=1, source_target_pairs={{0,16},{16,0},{1,17},{17,1},{2,18},{18,2},{3,19},{19,3},{4,20},{20... | collective-permute-start | bytes 3145736 | tf_op jit(solution)/shard_map/ppermute | solution.py:105
  155.2 74.7 %collective-permute-start.26 = (bf16[2048,256]{1,0:T(8,128)(2,1)}, bf16[2048,256]{1,0:T(8,128)(2,1)}, u32[]{:S(2)}, u32[]{:S(2)}) collective-permute-start(bf16[2048,256]{1,0:T(8,128)(2,1)} %pad_maximum_fusion.19), channel_id=1, source_target_pairs={{0,16},{16,0},{1,17},{17,1},{2,18},{18,2},{3,19},{19,3},{4,20},{20... | collective-permute-start | bytes 3145736 | tf_op jit(solution)/shard_map/ppermute | solution.py:105
  164.2 98.9 %collective-permute-start.52 = (bf16[256,2048]{1,0:T(8,128)(2,1)}, bf16[256,2048]{1,0:T(8,128)(2,1)}, u32[]{:S(2)}, u32[]{:S(2)}) collective-permute-start(bf16[256,2048]{1,0:T(8,128)(2,1)} %collective-permute-done.51), channel_id=1, source_target_pairs={{0,1},{1,2},{2,3},{3,0},{4,5},{5,6},{6,7},{7,4},{8,9},{9,10},{10,1... | collective-permute-start | bytes 3145736 | tf_op jit(solution)/shard_map/ppermute | solution.py:108
  181.8 55.4 %collective-permute-start.42 = (bf16[704,256]{1,0:T(8,128)(2,1)}, bf16[704,256]{1,0:T(8,128)(2,1)}, u32[]{:S(2)}, u32[]{:S(2)}) collective-permute-start(bf16[704,256]{1,0:T(8,128)(2,1)} %get-tuple-element.399), channel_id=1, source_target_pairs={{0,4},{4,0},{8,12},{12,8},{1,5},{5,1},{9,13},{13,9},{2,6},{6,2},{1... | collective-permute-start | bytes 1081352 | tf_op jit(solution)/shard_map/ppermute | solution.py:102
  264.6 49.6 %collective-permute-start.53 = (bf16[256,2048]{1,0:T(8,128)(2,1)}, bf16[256,2048]{1,0:T(8,128)(2,1)S(1)}, u32[]{:S(2)}, u32[]{:S(2)}) collective-permute-start(bf16[256,2048]{1,0:T(8,128)(2,1)} %collective-permute-done.52), channel_id=1, source_target_pairs={{0,1},{1,2},{2,3},{3,0},{4,5},{5,6},{6,7},{7,4},{8,9},{9,10},{10,1... | collective-permute-start | bytes 3145736 | tf_op jit(solution)/shard_map/ppermute | solution.py:108
  333.5 36.1 %collective-permute-start.57 = (bf16[256,2048]{1,0:T(8,128)(2,1)S(1)}, bf16[256,2048]{1,0:T(8,128)(2,1)S(1)}, u32[]{:S(2)}, u32[]{:S(2)}) collective-permute-start(bf16[256,2048]{1,0:T(8,128)(2,1)S(1)} %fusion.41), channel_id=1, source_target_pairs={{0,1},{1,2},{2,3},{3,0},{4,5},{5,6},{6,7},{7,4},{8,9},{9,10},{10,1... | collective-permute-start | bytes 3145736 | tf_op jit(solution)/shard_map/ppermute | solution.py:108
  347.2 44.9 %collective-permute-start.56 = (bf16[256,2048]{1,0:T(8,128)(2,1)S(1)}, bf16[256,2048]{1,0:T(8,128)(2,1)S(1)}, u32[]{:S(2)}, u32[]{:S(2)}) collective-permute-start(bf16[256,2048]{1,0:T(8,128)(2,1)S(1)} %collective-permute-done.55), channel_id=1, source_target_pairs={{0,1},{1,2},{2,3},{3,0},{4,5},{5,6},{6,7},{7,4},{8,9},{9,10},{10,1... | collective-permute-start | bytes 3145736 | tf_op jit(solution)/shard_map/ppermute | solution.py:108
  374.2 39.1 %collective-permute-start.58 = (bf16[256,2048]{1,0:T(8,128)(2,1)S(1)}, bf16[256,2048]{1,0:T(8,128)(2,1)S(1)}, u32[]{:S(2)}, u32[]{:S(2)}) collective-permute-start(bf16[256,2048]{1,0:T(8,128)(2,1)S(1)} %fusion.45), channel_id=1, source_target_pairs={{0,1},{1,2},{2,3},{3,0},{4,5},{5,6},{6,7},{7,4},{8,9},{9,10},{10,1... | collective-permute-start | bytes 3145736 | tf_op jit(solution)/shard_map/ppermute | solution.py:108
  418.8 56.0 %collective-permute-start.59 = (bf16[256,2048]{1,0:T(8,128)(2,1)}, bf16[256,2048]{1,0:T(8,128)(2,1)S(1)}, u32[]{:S(2)}, u32[]{:S(2)}) collective-permute-start(bf16[256,2048]{1,0:T(8,128)(2,1)} %fusion.46), channel_id=1, source_target_pairs={{0,1},{1,2},{2,3},{3,0},{4,5},{5,6},{6,7},{7,4},{8,9},{9,10},{10,1... | collective-permute-start | bytes 3145736 | tf_op jit(solution)/shard_map/ppermute | solution.py:108
  437.8 272.2 %collective-permute-start.96 = (bf16[1024,1408]{1,0:T(8,128)(2,1)}, bf16[1024,1408]{1,0:T(8,128)(2,1)}, u32[]{:S(2)}, u32[]{:S(2)}) collective-permute-start(bf16[1024,1408]{1,0:T(8,128)(2,1)} %pad_maximum_fusion.1), channel_id=1, source_target_pairs={{0,16},{16,0},{1,17},{17,1},{2,18},{18,2},{3,19},{19,3},{4,20},{20... | collective-permute-start | bytes 8650760 | tf_op jit(solution)/shard_map/ppermute | solution.py:105
  457.2 259.5 %collective-permute-start.99 = (bf16[1024,1408]{1,0:T(8,128)(2,1)}, bf16[1024,1408]{1,0:T(8,128)(2,1)}, u32[]{:S(2)}, u32[]{:S(2)}) collective-permute-start(bf16[1024,1408]{1,0:T(8,128)(2,1)} %pad_maximum_fusion.2), channel_id=1, source_target_pairs={{0,16},{16,0},{1,17},{17,1},{2,18},{18,2},{3,19},{19,3},{4,20},{20... | collective-permute-start | bytes 8650760 | tf_op jit(solution)/shard_map/ppermute | solution.py:105
  470.7 196.2 %collective-permute-start.105 = (bf16[704,1024]{1,0:T(8,128)(2,1)}, bf16[704,1024]{1,0:T(8,128)(2,1)}, u32[]{:S(2)}, u32[]{:S(2)}) collective-permute-start(bf16[704,1024]{1,0:T(8,128)(2,1)} %pad_maximum_fusion.10), channel_id=1, source_target_pairs={{0,16},{16,0},{1,17},{17,1},{2,18},{18,2},{3,19},{19,3},{4,20},{20... | collective-permute-start | bytes 4325384 | tf_op jit(solution)/shard_map/ppermute | solution.py:105
  562.9 106.1 %collective-permute-start.102 = (bf16[704,1024]{1,0:T(8,128)(2,1)}, bf16[704,1024]{1,0:T(8,128)(2,1)}, u32[]{:S(2)}, u32[]{:S(2)}) collective-permute-start(bf16[704,1024]{1,0:T(8,128)(2,1)} %pad_maximum_fusion.9), channel_id=1, source_target_pairs={{0,16},{16,0},{1,17},{17,1},{2,18},{18,2},{3,19},{19,3},{4,20},{20... | collective-permute-start | bytes 4325384 | tf_op jit(solution)/shard_map/ppermute | solution.py:105
  563.4 116.5 %collective-permute-start.60 = (bf16[256,2048]{1,0:T(8,128)(2,1)}, bf16[256,2048]{1,0:T(8,128)(2,1)}, u32[]{:S(2)}, u32[]{:S(2)}) collective-permute-start(bf16[256,2048]{1,0:T(8,128)(2,1)} %convolution_convert_fusion.7), channel_id=1, source_target_pairs={{0,1},{1,2},{2,3},{3,0},{4,5},{5,6},{6,7},{7,4},{8,9},{9,10},{10,1... | collective-permute-start | bytes 3145736 | tf_op jit(solution)/shard_map/ppermute | solution.py:108
  694.4 49.6 %collective-permute-start.65 = (bf16[1024,1024]{1,0:T(8,128)(2,1)}, bf16[1024,1024]{1,0:T(8,128)(2,1)}, u32[]{:S(2)}, u32[]{:S(2)}) collective-permute-start(bf16[1024,1024]{1,0:T(8,128)(2,1)} %pad_maximum_fusion.3), channel_id=1, source_target_pairs={{0,16},{16,0},{1,17},{17,1},{2,18},{18,2},{3,19},{19,3},{4,20},{20... | collective-permute-start | bytes 6291464 | tf_op jit(solution)/shard_map/ppermute | solution.py:105
  707.8 49.2 %collective-permute-start.68 = (bf16[1024,1024]{1,0:T(8,128)(2,1)}, bf16[1024,1024]{1,0:T(8,128)(2,1)S(1)}, u32[]{:S(2)}, u32[]{:S(2)}) collective-permute-start(bf16[1024,1024]{1,0:T(8,128)(2,1)} %pad_maximum_fusion.4), channel_id=1, source_target_pairs={{0,16},{16,0},{1,17},{17,1},{2,18},{18,2},{3,19},{19,3},{4,20},{20... | collective-permute-start | bytes 6291464 | tf_op jit(solution)/shard_map/ppermute | solution.py:105
  708.4 41.1 %collective-permute-start.87 = (bf16[1024,1024]{0,1:T(8,128)(2,1)}, bf16[1024,1024]{0,1:T(8,128)(2,1)}, u32[]{:S(2)}, u32[]{:S(2)}) collective-permute-start(bf16[1024,1024]{0,1:T(8,128)(2,1)} %pad_maximum_fusion.5), channel_id=1, source_target_pairs={{0,16},{16,0},{1,17},{17,1},{2,18},{18,2},{3,19},{19,3},{4,20},{20... | collective-permute-start | bytes 6291464 | tf_op jit(solution)/shard_map/ppermute | solution.py:105
  744.0 120.0 %collective-permute-start.97 = (bf16[512,1408]{1,0:T(8,128)(2,1)}, bf16[512,1408]{1,0:T(8,128)(2,1)}, u32[]{:S(2)}, u32[]{:S(2)}) collective-permute-start(bf16[512,1408]{1,0:T(8,128)(2,1)} %pad_maximum_fusion.8), channel_id=1, source_target_pairs={{0,4},{4,0},{8,12},{12,8},{1,5},{5,1},{9,13},{13,9},{2,6},{6,2},{1... | collective-permute-start | bytes 4325384 | tf_op jit(solution)/shard_map/ppermute | solution.py:102
  749.3 47.0 %collective-permute-start.62 = (bf16[256,2048]{1,0:T(8,128)(2,1)}, bf16[256,2048]{1,0:T(8,128)(2,1)}, u32[]{:S(2)}, u32[]{:S(2)}) collective-permute-start(bf16[256,2048]{1,0:T(8,128)(2,1)} %fusion.42), channel_id=1, source_target_pairs={{0,1},{1,2},{2,3},{3,0},{4,5},{5,6},{6,7},{7,4},{8,9},{9,10},{10,1... | collective-permute-start | bytes 3145736 | tf_op jit(solution)/shard_map/ppermute | solution.py:108
  757.1 37.3 %collective-permute-start.78 = (bf16[256,512]{1,0:T(8,128)(2,1)S(1)}, bf16[256,512]{1,0:T(8,128)(2,1)S(1)}, u32[]{:S(2)}, u32[]{:S(2)}) collective-permute-start(bf16[256,512]{1,0:T(8,128)(2,1)S(1)} %fusion.95), channel_id=1, source_target_pairs={{0,2},{1,3},{2,0},{3,1},{4,6},{5,7},{6,4},{7,5},{8,10},{9,11},{10,... | collective-permute-start | bytes 786440 | tf_op jit(solution)/shard_map/ppermute | solution.py:114
  794.4 51.4 %collective-permute-start.69 = (bf16[512,1024]{1,0:T(8,128)(2,1)S(1)}, bf16[512,1024]{1,0:T(8,128)(2,1)S(1)}, u32[]{:S(2)}, u32[]{:S(2)}) collective-permute-start(bf16[512,1024]{1,0:T(8,128)(2,1)S(1)} %pad_maximum_fusion.22), channel_id=1, source_target_pairs={{0,4},{4,0},{8,12},{12,8},{1,5},{5,1},{9,13},{13,9},{2,6},{6,2},{1... | collective-permute-start | bytes 3145736 | tf_op jit(solution)/shard_map/ppermute | solution.py:102
  796.3 58.2 %collective-permute-start.91 = (bf16[1024,512]{0,1:T(8,128)(2,1)}, bf16[1024,512]{0,1:T(8,128)(2,1)S(1)}, u32[]{:S(2)}, u32[]{:S(2)}) collective-permute-start(bf16[1024,512]{0,1:T(8,128)(2,1)} %pad_maximum_fusion.24), channel_id=1, source_target_pairs={{0,4},{4,0},{8,12},{12,8},{1,5},{5,1},{9,13},{13,9},{2,6},{6,2},{1... | collective-permute-start | bytes 3145736 | tf_op jit(solution)/shard_map/ppermute | solution.py:102
  809.2 36.6 %collective-permute-start.80 = (bf16[256,512]{1,0:T(8,128)(2,1)S(1)}, bf16[256,512]{1,0:T(8,128)(2,1)S(1)}, u32[]{:S(2)}, u32[]{:S(2)}) collective-permute-start(bf16[256,512]{1,0:T(8,128)(2,1)S(1)} %add_convert_fusion.2), channel_id=1, source_target_pairs={{0,4},{4,0},{8,12},{12,8},{1,5},{5,1},{9,13},{13,9},{2,6},{6,2},{1... | collective-permute-start | bytes 786440 | tf_op jit(solution)/shard_map/ppermute | solution.py:102
  857.8 43.9 %collective-permute-start.70 = (bf16[256,1024]{1,0:T(8,128)(2,1)}, bf16[256,1024]{1,0:T(8,128)(2,1)S(1)}, u32[]{:S(2)}, u32[]{:S(2)}) collective-permute-start(bf16[256,1024]{1,0:T(8,128)(2,1)} %fusion.74), channel_id=1, source_target_pairs={{0,8},{4,12},{8,0},{12,4},{1,9},{5,13},{9,1},{13,5},{2,10},{6,14},... | collective-permute-start | bytes 1572872 | tf_op jit(solution)/shard_map/ppermute | solution.py:102
  858.4 45.4 %collective-permute-start.89 = (bf16[1024,256]{0,1:T(8,128)(2,1)S(1)}, bf16[1024,256]{0,1:T(8,128)(2,1)S(1)}, u32[]{:S(2)}, u32[]{:S(2)}) collective-permute-start(bf16[1024,256]{0,1:T(8,128)(2,1)S(1)} %fusion.71), channel_id=1, source_target_pairs={{0,4},{4,0},{8,12},{12,8},{1,5},{5,1},{9,13},{13,9},{2,6},{6,2},{1... | collective-permute-start | bytes 1572872 | tf_op jit(solution)/shard_map/ppermute | solution.py:102
  864.0 49.0 %collective-permute-start.92 = (bf16[1024,256]{0,1:T(8,128)(2,1)S(1)}, bf16[1024,256]{0,1:T(8,128)(2,1)S(1)}, u32[]{:S(2)}, u32[]{:S(2)}) collective-permute-start(bf16[1024,256]{0,1:T(8,128)(2,1)S(1)} %copy-done.130), channel_id=1, source_target_pairs={{0,8},{4,12},{8,0},{12,4},{1,9},{5,13},{9,1},{13,5},{2,10},{6,14},... | collective-permute-start | bytes 1572872 | tf_op jit(solution)/shard_map/ppermute | solution.py:102
  890.5 57.0 %collective-permute-start.98 = (bf16[256,1408]{1,0:T(8,128)(2,1)S(1)}, bf16[256,1408]{1,0:T(8,128)(2,1)}, u32[]{:S(2)}, u32[]{:S(2)}) collective-permute-start(bf16[256,1408]{1,0:T(8,128)(2,1)S(1)} %fusion.59), channel_id=1, source_target_pairs={{0,8},{4,12},{8,0},{12,4},{1,9},{5,13},{9,1},{13,5},{2,10},{6,14},... | collective-permute-start | bytes 2162696 | tf_op jit(solution)/shard_map/ppermute | solution.py:102
  892.9 57.7 %collective-permute-start.101 = (bf16[256,1408]{1,0:T(8,128)(2,1)}, bf16[256,1408]{1,0:T(8,128)(2,1)}, u32[]{:S(2)}, u32[]{:S(2)}) collective-permute-start(bf16[256,1408]{1,0:T(8,128)(2,1)} %fusion.57), channel_id=1, source_target_pairs={{0,4},{4,0},{8,12},{12,8},{1,5},{5,1},{9,13},{13,9},{2,6},{6,2},{1... | collective-permute-start | bytes 2162696 | tf_op jit(solution)/shard_map/ppermute | solution.py:102
  (259 other events, 3536.7 us)
